TPU v7x, 32 devices: a whole 2x2x4 slice. The times are simulated.
32 devices in a mesh: grp: 8 (over z, core), own: 4 (over y, x).
Axes of the slice: x: 2, y: 2, z: 4, core: 2. Of those that a mesh axis runs over, the one named last changes fastest.
Arguments:
- tokens: bfloat16 [8192, 1024], P(('grp', 'own')), may hold values from -6 to 6
- cotangent: bfloat16 [8192, 1024], P(('grp', 'own')), may hold values from -6 to 6
- doc_lengths: int32 [4, 4], replicated, may hold values from 256 to 1280, as said below
- w_in: float32 [1024, 3072], P('own', 'grp'), may hold values from -0.1875 to 0.1875
- w_out: float32 [1024, 1024], P('own', 'grp'), may hold values from -0.1875 to 0.1875
- w_gate: float32 [1024, 4608], P('own', 'grp'), may hold values from -0.1875 to 0.1875
- w_up: float32 [1024, 4608], P('own', 'grp'), may hold values from -0.1875 to 0.1875
- w_down: float32 [4608, 1024], P('own', 'grp'), may hold values from -0.09375 to 0.09375
- conv_w: float32 [3, 1024], P(None, 'own'), may hold values from -3.5 to 3.5
- gain: float32 [1024], P('own'), may hold values from 0.5 to 1.5
- gain_two: float32 [1024], P('own'), may hold values from 0.5 to 1.5
- moment_in: float32 [1024, 3072], P('own', 'grp'), as said below
- moment_out: float32 [1024, 1024], P('own', 'grp'), as said below
- moment_gate: float32 [1024, 4608], P('own', 'grp'), as said below
- moment_up: float32 [1024, 4608], P('own', 'grp'), as said below
- moment_down: float32 [4608, 1024], P('own', 'grp'), as said below
- moment_conv: float32 [3, 1024], P(None, 'own'), as said below
- moment_gain: float32 [1024], P('own'), as said below
- moment_gain_two: float32 [1024], P('own'), as said below
- square_in: float32 [1024, 3072], P('own', 'grp'), as said below
- square_out: float32 [1024, 1024], P('own', 'grp'), as said below
- square_gate: float32 [1024, 4608], P('own', 'grp'), as said below
- square_up: float32 [1024, 4608], P('own', 'grp'), as said below
- square_down: float32 [4608, 1024], P('own', 'grp'), as said below
- square_conv: float32 [3, 1024], P(None, 'own'), as said below
- square_gain: float32 [1024], P('own'), as said below
- square_gain_two: float32 [1024], P('own'), as said below
Outputs:
- block_out: bfloat16 [8192, 1024], P(('grp', 'own'))
- grad_tokens: bfloat16 [8192, 1024], P(('grp', 'own'))
- grad_w_in: float32 [1024, 3072], P('own')
- grad_w_out: float32 [1024, 1024], P('own')
- grad_w_gate: float32 [1024, 4608], P('own')
- grad_w_up: float32 [1024, 4608], P('own')
- grad_w_down: float32 [4608, 1024], P('own')
- grad_conv_w: float32 [3, 1024], P(None, 'own')
- grad_gain: float32 [1024], P('own')
- grad_gain_two: float32 [1024], P('own')
- new_w_in: float32 [1024, 3072], P('own', 'grp')
- new_w_out: float32 [1024, 1024], P('own', 'grp')
- new_w_gate: float32 [1024, 4608], P('own', 'grp')
- new_w_up: float32 [1024, 4608], P('own', 'grp')
- new_w_down: float32 [4608, 1024], P('own', 'grp')
- new_conv_w: float32 [3, 1024], P(None, 'own')
- new_gain: float32 [1024], P('own')
- new_gain_two: float32 [1024], P('own')
- new_moment_in: float32 [1024, 3072], P('own', 'grp')
- new_moment_out: float32 [1024, 1024], P('own', 'grp')
- new_moment_gate: float32 [1024, 4608], P('own', 'grp')
- new_moment_up: float32 [1024, 4608], P('own', 'grp')
- new_moment_down: float32 [4608, 1024], P('own', 'grp')
- new_moment_conv: float32 [3, 1024], P(None, 'own')
- new_moment_gain: float32 [1024], P('own')
- new_moment_gain_two: float32 [1024], P('own')
- new_square_in: float32 [1024, 3072], P('own', 'grp')
- new_square_out: float32 [1024, 1024], P('own', 'grp')
- new_square_gate: float32 [1024, 4608], P('own', 'grp')
- new_square_up: float32 [1024, 4608], P('own', 'grp')
- new_square_down: float32 [4608, 1024], P('own', 'grp')
- new_square_conv: float32 [3, 1024], P(None, 'own')
- new_square_gain: float32 [1024], P('own')
- new_square_gain_two: float32 [1024], P('own')
Inputs may be any that keep to these rules, and one draw needn't show every extreme that they name: `doc_lengths`: the 4 lengths of each sequence sum to 2048. `moment_in`: first moments: real values of either sign. `moment_out`: first moments: real values of either sign. `moment_gate`: first moments: real values of either sign. `moment_up`: first moments: real values of either sign. `moment_down`: first moments: real values of either sign. `moment_conv`: first moments: real values of either sign. `moment_gain`: first moments: real values of either sign. `moment_gain_two`: first moments: real values of either sign. `square_in`: second moments are positive. `square_out`: second moments are positive. `square_gate`: second moments are positive. `square_up`: second moments are positive. `square_down`: second moments are positive. `square_conv`: second moments are positive. `square_gain`: second moments are positive. `square_gain_two`: second moments are positive.
All inputs are finite; a program needn't handle non-finite values.
Results may differ from a plain program's by a relative error of at most 0.025.
Values may be sent and summed in bfloat16 or wider, within the bound.
No kernel may reach another device: no remote copies, remote signals or barrier semaphores. Data moves between devices by JAX's collectives and lax.ppermute only.
A program may use at most 320 MiB of HBM per device.

v0:
```python
import jax
import jax.numpy as jnp
from jax import lax
from jax.sharding import PartitionSpec as P

SEQ_LEN = 2048
eps_norm = 1e-05
eps_adam = 1e-08
beta_one = 0.9
beta_two = 0.95
train_step = 5
rate_matrix = 0.004
rate_vector = 0.1
decay_matrix = 0.1


def passed_along(block, axis, distance):
    devices = range(lax.axis_size(axis))
    route = [(i - distance, i) for i in devices if i - distance in devices]
    return lax.ppermute(block, axis, route)


def stream_starts(doc_lengths, seq_len):
    starts = jnp.cumsum(doc_lengths, axis=1) - doc_lengths
    base = (jnp.arange(doc_lengths.shape[0], dtype=jnp.int32) * seq_len)[:, None]
    first = (jnp.arange(doc_lengths.shape[1], dtype=jnp.int32) == 0)[None, :]
    return jnp.where(first, 0, base + starts).reshape(-1)


def since_start(positions, stream):
    below = jnp.where(stream[None, :] <= positions[:, None], stream[None, :], 0)
    return positions - jnp.max(below, axis=1)


def apply_adam(param, first, second, grad, rate, decay):
    first_new = beta_one * first + (1.0 - beta_one) * grad
    second_new = beta_two * second + (1.0 - beta_two) * grad * grad
    first_hat = first_new / (1.0 - beta_one**train_step)
    second_hat = second_new / (1.0 - beta_two**train_step)
    param_new = param - rate * (first_hat / (jnp.sqrt(second_hat) + eps_adam) + decay * param)
    return (param_new, first_new, second_new)


def local(
    tokens,
    cotangent,
    doc_lengths,
    w_in,
    w_out,
    w_gate,
    w_up,
    w_down,
    conv_w,
    gain,
    gain_two,
    moment_in,
    moment_out,
    moment_gate,
    moment_up,
    moment_down,
    moment_conv,
    moment_gain,
    moment_gain_two,
    square_in,
    square_out,
    square_gate,
    square_up,
    square_down,
    square_conv,
    square_gain,
    square_gain_two,
):
    across = (
        lax.all_gather(w_in.astype(jnp.bfloat16), "grp", axis=1, tiled=True),
        lax.all_gather(w_out.astype(jnp.bfloat16), "grp", axis=1, tiled=True),
        lax.all_gather(w_gate.astype(jnp.bfloat16), "grp", axis=1, tiled=True),
        lax.all_gather(w_up.astype(jnp.bfloat16), "grp", axis=1, tiled=True),
        lax.all_gather(w_down.astype(jnp.bfloat16), "grp", axis=1, tiled=True),
    )
    in_half, out_half, gate_half, up_half, down_half, conv_half, gain_half, gain_two_half = (
        lax.all_gather(across[0], "own", axis=0, tiled=True),
        lax.all_gather(across[1], "own", axis=0, tiled=True),
        lax.all_gather(across[2], "own", axis=0, tiled=True),
        lax.all_gather(across[3], "own", axis=0, tiled=True),
        lax.all_gather(across[4], "own", axis=0, tiled=True),
        lax.all_gather(conv_w.astype(jnp.bfloat16), "own", axis=1, tiled=True),
        lax.all_gather(gain.astype(jnp.bfloat16), "own", axis=0, tiled=True),
        lax.all_gather(gain_two.astype(jnp.bfloat16), "own", axis=0, tiled=True),
    )
    conv_float = conv_half.astype(jnp.float32)
    gain_float = gain_half.astype(jnp.float32)
    gain_two_float = gain_two_half.astype(jnp.float32)
    rows, width = tokens.shape
    hidden_width = gate_half.shape[1]
    taps = conv_half.shape[0]
    device = lax.axis_index(("grp", "own"))
    first_row = device * rows
    stream = stream_starts(doc_lengths, SEQ_LEN)
    position = first_row + jnp.arange(rows + taps - 1, dtype=jnp.int32)
    since = since_start(position, stream)
    x_float = tokens.astype(jnp.float32)
    cot_float = cotangent.astype(jnp.float32)
    inv_rms = lax.rsqrt(jnp.mean(x_float * x_float, axis=1, keepdims=True) + eps_norm)
    normed = (x_float * inv_rms * gain_float).astype(jnp.bfloat16)
    project = jnp.dot(normed, in_half, preferred_element_type=jnp.float32)
    b_gate = project[:, :width]
    c_gate = project[:, width : 2 * width]
    x_value = project[:, 2 * width :]
    gated = b_gate * x_value
    before = passed_along(gated[rows - taps + 1 :], ("grp", "own"), 1)
    extended = jnp.concatenate([before, gated], 0)
    convolved = jnp.zeros((rows, width), jnp.float32)
    for tap_index in range(taps):
        keep = (since[:rows] >= tap_index)[:, None]
        moved = extended[taps - 1 - tap_index : taps - 1 - tap_index + rows]
        convolved = convolved + jnp.where(keep, conv_float[tap_index] * moved, 0.0)
    mixed = (c_gate * convolved).astype(jnp.bfloat16)
    middle = x_float + jnp.dot(mixed, out_half, preferred_element_type=jnp.float32)
    inv_two = lax.rsqrt(jnp.mean(middle * middle, axis=1, keepdims=True) + eps_norm)
    normed_two = (middle * inv_two * gain_two_float).astype(jnp.bfloat16)
    gate = jnp.dot(normed_two, gate_half, preferred_element_type=jnp.float32)
    up = jnp.dot(normed_two, up_half, preferred_element_type=jnp.float32)
    sig = jax.nn.sigmoid(gate)
    activated = gate * sig
    hidden = (activated * up).astype(jnp.bfloat16)
    block_out = (middle + jnp.dot(hidden, down_half, preferred_element_type=jnp.float32)).astype(
        jnp.bfloat16
    )
    grad_hidden = jnp.dot(cotangent, down_half.T, preferred_element_type=jnp.float32)
    grad_gate = (grad_hidden * up * sig * (1.0 + gate * (1.0 - sig))).astype(jnp.bfloat16)
    grad_up = (grad_hidden * activated).astype(jnp.bfloat16)
    grad_normed_two = jnp.dot(grad_gate, gate_half.T, preferred_element_type=jnp.float32) + jnp.dot(
        grad_up, up_half.T, preferred_element_type=jnp.float32
    )
    gain_two_rows = jnp.sum(grad_normed_two * middle * inv_two, axis=0)
    weighted_two = gain_two_float * grad_normed_two
    grad_middle = (
        cot_float
        + inv_two * weighted_two
        - middle
        * inv_two
        * inv_two
        * inv_two
        * jnp.mean(weighted_two * middle, axis=1, keepdims=True)
    )
    grad_middle_half = grad_middle.astype(jnp.bfloat16)
    grad_mixed = jnp.dot(grad_middle_half, out_half.T, preferred_element_type=jnp.float32)
    grad_c = grad_mixed * convolved
    grad_conv = grad_mixed * c_gate
    after = passed_along(grad_conv[: taps - 1], ("grp", "own"), -1)
    grad_extended = jnp.concatenate([grad_conv, after], 0)
    grad_gated = jnp.zeros((rows, width), jnp.float32)
    tap_sums = []
    for tap_index in range(taps):
        keep_ahead = (since[tap_index : tap_index + rows] >= tap_index)[:, None]
        grad_gated = grad_gated + conv_float[tap_index] * jnp.where(
            keep_ahead, grad_extended[tap_index : tap_index + rows], 0.0
        )
        keep = (since[:rows] >= tap_index)[:, None]
        moved = extended[taps - 1 - tap_index : taps - 1 - tap_index + rows]
        tap_sums.append(jnp.sum(jnp.where(keep, grad_conv * moved, 0.0), axis=0))
    grad_b = grad_gated * x_value
    grad_x = grad_gated * b_gate
    grad_project = jnp.concatenate([grad_b, grad_c, grad_x], 1).astype(jnp.bfloat16)
    grad_normed = jnp.dot(grad_project, in_half.T, preferred_element_type=jnp.float32)
    gain_rows = jnp.sum(grad_normed * x_float * inv_rms, axis=0)
    weighted = gain_float * grad_normed
    grad_tokens = (
        grad_middle
        + inv_rms * weighted
        - x_float
        * inv_rms
        * inv_rms
        * inv_rms
        * jnp.mean(weighted * x_float, axis=1, keepdims=True)
    ).astype(jnp.bfloat16)
    small_terms = jnp.stack(tap_sums + [gain_rows, gain_two_rows], axis=1)
    wide_terms = jnp.concatenate(
        [
            jnp.dot(normed.T, grad_project, preferred_element_type=jnp.float32),
            jnp.dot(mixed.T, grad_middle_half, preferred_element_type=jnp.float32),
            jnp.dot(normed_two.T, grad_gate, preferred_element_type=jnp.float32),
            jnp.dot(normed_two.T, grad_up, preferred_element_type=jnp.float32),
        ],
        1,
    )
    down_terms = jnp.dot(hidden.T, cotangent, preferred_element_type=jnp.float32)
    shares = (
        lax.psum_scatter(
            wide_terms.astype(jnp.bfloat16), "own", scatter_dimension=0, tiled=True
        ).astype(jnp.float32),
        lax.psum_scatter(
            down_terms.astype(jnp.bfloat16), "own", scatter_dimension=0, tiled=True
        ).astype(jnp.float32),
        lax.psum_scatter(
            small_terms.astype(jnp.bfloat16), "own", scatter_dimension=0, tiled=True
        ).astype(jnp.float32),
    )
    wide_share, down_share, small_share = (
        lax.psum(shares[0].astype(jnp.bfloat16), "grp").astype(jnp.float32),
        lax.psum(shares[1].astype(jnp.bfloat16), "grp").astype(jnp.float32),
        lax.psum(shares[2].astype(jnp.bfloat16), "grp").astype(jnp.float32),
    )
    grad_w_in = wide_share[:, : 3 * width]
    grad_w_out = wide_share[:, 3 * width : 4 * width]
    grad_w_gate = wide_share[:, 4 * width : 4 * width + hidden_width]
    grad_w_up = wide_share[:, 4 * width + hidden_width :]
    grad_conv_w = small_share[:, :taps].T
    grad_gain = small_share[:, taps]
    grad_gain_two = small_share[:, taps + 1]
    column = lax.axis_index("grp")

    def own_columns(grad, param):
        count = param.shape[1]
        return lax.dynamic_slice_in_dim(grad, column * count, count, 1)

    new_w_in, new_moment_in, new_square_in = apply_adam(
        w_in, moment_in, square_in, own_columns(grad_w_in, w_in), rate_matrix, decay_matrix
    )
    new_w_out, new_moment_out, new_square_out = apply_adam(
        w_out, moment_out, square_out, own_columns(grad_w_out, w_out), rate_matrix, decay_matrix
    )
    new_w_gate, new_moment_gate, new_square_gate = apply_adam(
        w_gate,
        moment_gate,
        square_gate,
        own_columns(grad_w_gate, w_gate),
        rate_matrix,
        decay_matrix,
    )
    new_w_up, new_moment_up, new_square_up = apply_adam(
        w_up, moment_up, square_up, own_columns(grad_w_up, w_up), rate_matrix, decay_matrix
    )
    new_w_down, new_moment_down, new_square_down = apply_adam(
        w_down, moment_down, square_down, own_columns(down_share, w_down), rate_matrix, decay_matrix
    )
    new_conv_w, new_moment_conv, new_square_conv = apply_adam(
        conv_w, moment_conv, square_conv, grad_conv_w, rate_vector, 0.0
    )
    new_gain, new_moment_gain, new_square_gain = apply_adam(
        gain, moment_gain, square_gain, grad_gain, rate_vector, 0.0
    )
    new_gain_two, new_moment_gain_two, new_square_gain_two = apply_adam(
        gain_two, moment_gain_two, square_gain_two, grad_gain_two, rate_vector, 0.0
    )
    return (
        block_out,
        grad_tokens,
        grad_w_in,
        grad_w_out,
        grad_w_gate,
        grad_w_up,
        down_share,
        grad_conv_w,
        grad_gain,
        grad_gain_two,
        new_w_in,
        new_w_out,
        new_w_gate,
        new_w_up,
        new_w_down,
        new_conv_w,
        new_gain,
        new_gain_two,
        new_moment_in,
        new_moment_out,
        new_moment_gate,
        new_moment_up,
        new_moment_down,
        new_moment_conv,
        new_moment_gain,
        new_moment_gain_two,
        new_square_in,
        new_square_out,
        new_square_gate,
        new_square_up,
        new_square_down,
        new_square_conv,
        new_square_gain,
        new_square_gain_two,
    )


def solution(mesh):
    placed = (
        P(("grp", "own"), None),
        P(("grp", "own"), None),
        P(),
        P("own", "grp"),
        P("own", "grp"),
        P("own", "grp"),
        P("own", "grp"),
        P("own", "grp"),
        P(None, "own"),
        P("own"),
        P("own"),
        P("own", "grp"),
        P("own", "grp"),
        P("own", "grp"),
        P("own", "grp"),
        P("own", "grp"),
        P(None, "own"),
        P("own"),
        P("own"),
        P("own", "grp"),
        P("own", "grp"),
        P("own", "grp"),
        P("own", "grp"),
        P("own", "grp"),
        P(None, "own"),
        P("own"),
        P("own"),
    )
    return jax.shard_map(
        local,
        mesh=mesh,
        in_specs=placed,
        out_specs=(
            P(("grp", "own"), None),
            P(("grp", "own"), None),
            P("own", None),
            P("own", None),
            P("own", None),
            P("own", None),
            P("own", None),
            P(None, "own"),
            P("own"),
            P("own"),
            P("own", "grp"),
            P("own", "grp"),
            P("own", "grp"),
            P("own", "grp"),
            P("own", "grp"),
            P(None, "own"),
            P("own"),
            P("own"),
            P("own", "grp"),
            P("own", "grp"),
            P("own", "grp"),
            P("own", "grp"),
            P("own", "grp"),
            P(None, "own"),
            P("own"),
            P("own"),
            P("own", "grp"),
            P("own", "grp"),
            P("own", "grp"),
            P("own", "grp"),
            P("own", "grp"),
            P(None, "own"),
            P("own"),
            P("own"),
        ),
        check_vma=False,
    )
```

profile of v0, /device:TPU:0, one launch (start us, length us, event | category | flops | bytes accessed | tf_op | source)
XLA Modules:
  0.0 1173.6 jit_solution(15216509789549518167)
XLA Ops:
  14.7 23.3 %all-gather.12.cloned.1.call-done = bf16[256,3072]{1,0:T(8,128)(2,1)} async-done(((bf16[256,384]{1,0:T(8,128)(2,1)}), bf16[256,3072]{1,0:T(8,128)(2,1)}) %all-gather.12.cloned.1.call-update) | async-done | bytes 1572880 | tf_op jit(solution)/shard_map/all_gather | solution.py:74
  38.1 14.9 %all_gather.43 = bf16[256,1024]{1,0:T(8,128)(2,1)} all-gather(bf16[256,128]{1,0:T(8,128)(2,1)S(1)} %convert_element_type.95), channel_id=1, replica_groups=mesh['grp'=8,'own'=4] {'grp'}, dimensions={1}, use_global_device_ids=true | all-gather | bytes 589824 | tf_op jit(solution)/shard_map/all_gather | solution.py:75
  53.1 18.9 %all-gather.18.cloned.1.call-done = bf16[256,4608]{0,1:T(8,128)(2,1)} async-done(((bf16[256,576]{0,1:T(8,128)(2,1)}), bf16[256,4608]{0,1:T(8,128)(2,1)}) %all-gather.18.cloned.1.call-update) | async-done | bytes 2359312 | tf_op jit(solution)/shard_map/all_gather | solution.py:76
  72.1 32.5 %all-gather.22.cloned.1.call-done = bf16[256,4608]{0,1:T(8,128)(2,1)} async-done(((bf16[256,576]{0,1:T(8,128)(2,1)}), bf16[256,4608]{0,1:T(8,128)(2,1)}) %all-gather.22.cloned.1.call-update) | async-done | bytes 2359312 | tf_op jit(solution)/shard_map/all_gather | solution.py:77
  104.7 33.9 %all-gather.26.cloned.1.call-done = bf16[1152,1024]{1,0:T(8,128)(2,1)} async-done(((bf16[1152,128]{1,0:T(8,128)(2,1)}), bf16[1152,1024]{1,0:T(8,128)(2,1)}) %all-gather.26.cloned.1.call-update) | async-done | bytes 2359312 | tf_op jit(solution)/shard_map/all_gather | solution.py:78
  138.7 8.0 all-gather
  147.2 8.3 all_gather.42
  155.9 53.3 %all-gather.14.cloned.1.call-done = bf16[1024,3072]{1,0:T(8,128)(2,1)} async-done(((bf16[256,3072]{1,0:T(8,128)(2,1)}), bf16[1024,3072]{1,0:T(8,128)(2,1)}) %all-gather.14.cloned.1.call-update) | async-done | bytes 6291472 | tf_op jit(solution)/shard_map/all_gather | solution.py:81
  209.2 4.7 fusion.30
  214.0 3.4 collective-permute-start
  217.5 8.4 all-gather.1
  227.4 18.7 %all-gather.16.cloned.1.call-done = bf16[1024,1024]{1,0:T(8,128)(2,1)} async-done(((bf16[256,1024]{1,0:T(8,128)(2,1)}), bf16[1024,1024]{1,0:T(8,128)(2,1)}) %all-gather.16.cloned.1.call-update) | async-done | bytes 2097168 | tf_op jit(solution)/shard_map/all_gather | solution.py:82
  246.1 2.4 multiply_reduce_fusion.2
  248.7 95.3 %all-gather.20.cloned.1.call-done = bf16[1024,4608]{0,1:T(8,128)(2,1)} async-done(((bf16[256,4608]{0,1:T(8,128)(2,1)}), bf16[1024,4608]{0,1:T(8,128)(2,1)}) %all-gather.20.cloned.1.call-update) | async-done | bytes 9437200 | tf_op jit(solution)/shard_map/all_gather | solution.py:83
  344.0 11.5 fusion.51
  355.5 86.4 %all-gather.24.cloned.1.call-done = bf16[1024,4608]{0,1:T(8,128)(2,1)} async-done(((bf16[256,4608]{0,1:T(8,128)(2,1)}), bf16[1024,4608]{0,1:T(8,128)(2,1)}) %all-gather.24.cloned.1.call-update) | async-done | bytes 9437200 | tf_op jit(solution)/shard_map/all_gather | solution.py:84
  441.9 11.5 fusion.52
  453.5 86.5 %all-gather.28.cloned.1.call-done = bf16[4608,1024]{1,0:T(8,128)(2,1)} async-done(((bf16[1152,1024]{1,0:T(8,128)(2,1)}), bf16[4608,1024]{1,0:T(8,128)(2,1)}) %all-gather.28.cloned.1.call-update) | async-done | bytes 9437200 | tf_op jit(solution)/shard_map/all_gather | solution.py:85
  540.0 13.8 %multiply_convert_fusion = (bf16[256,4608]{1,0:T(8,128)(2,1)}, bf16[256,4608]{1,0:T(8,128)(2,1)}, bf16[256,4608]{1,0:T(8,128)(2,1)S(1)}) fusion(f32[256,4608]{1,0:T(8,128)} %fusion.51, f32[256,4608]{1,0:T(8,128)} %fusion.52, bf16[256,1024]{1,0:T(8,128)(2,1)S(1)} %copy-done.16, bf16[4608,1024]{1,0:T(8,128)(2,1)} %all-gather.28.cloned.1.call-done), kind=kOutput, calls=%fused_computation.5 | convolution fusion | flops 2433613824 | bytes 26476544 | tf_op jit(solution)/shard_map/dot_general | solution.py:129
  555.2 5.0 convolution_convert_fusion
  560.6 6.0 fusion.53
  566.6 5.9 multiply_reduce_fusion
  577.2 5.1 convolution_convert_fusion.1
  582.3 5.2 convolution_convert_fusion.2
  587.6 2.1 convolution_convert_fusion.4
  591.0 4.5 convolution_convert_fusion.3
  595.6 31.4 %pad_maximum_fusion = bf16[1024,13312]{0,1:T(8,128)(2,1)} fusion(bf16[1024,4608]{0,1:T(8,128)(2,1)} %convolution_convert_fusion.1, bf16[1024,4608]{0,1:T(8,128)(2,1)} %convolution_convert_fusion.2, bf16[1024,1024]{0,1:T(8,128)(2,1)} %convolution_convert_fusion.4, bf16[1024,3072]{0,1:T(8,128)(2,1)} %convolution_convert_fusion.3), kind=kLoop, calls=%fused_computation | loop fusion | flops 109051904 | bytes 54525952 | tf_op jit(solution)/shard_map/concatenate | solution.py:178
  627.4 6.6 fusion.18
  634.8 20.7 %reduce-scatter.6.cloned.1.call-done = bf16[1152,1024]{1,0:T(8,128)(2,1)} async-done(((bf16[4608,1024]{1,0:T(8,128)(2,1)}), bf16[1152,1024]{1,0:T(8,128)(2,1)}) %reduce-scatter.6.cloned.1.call-update) | async-done | bytes 2359312 | tf_op jit(solution)/shard_map/reduce_scatter | solution.py:192
  655.5 241.9 %reduce-scatter.4.cloned.1.call-done = bf16[256,13312]{0,1:T(8,128)(2,1)} async-done(((bf16[1024,13312]{0,1:T(8,128)(2,1)}), bf16[256,13312]{0,1:T(8,128)(2,1)}) %reduce-scatter.4.cloned.1.call-update) | async-done | bytes 6815760 | tf_op jit(solution)/shard_map/reduce_scatter | solution.py:189
  899.0 1.9 copy.109
  900.9 1.9 copy.110
  906.2 7.9 fusion.1
  915.3 8.1 reduce-scatter.8.cloned.1.call-done
  923.4 16.4 %psum.23 = bf16[256,5]{0,1:T(8,128)(2,1)S(1)} all-reduce(bf16[256,5]{0,1:T(8,128)(2,1)} %reduce-scatter.8.cloned.1.call-done), channel_id=1, replica_groups=mesh['grp'=8,'own'=4] {'grp'}, use_global_device_ids=true, to_apply=%region_16.17 | all-reduce | flops 1280 | bytes 5120 | tf_op jit(solution)/shard_map/psum | solution.py:202
  941.1 175.2 %all-reduce.3.cloned.1.call-done = (bf16[256,13312]{0,1:T(8,128)(2,1)}, bf16[1152,1024]{1,0:T(8,128)(2,1)}) async-done(((bf16[256,13312]{0,1:T(8,128)(2,1)}, bf16[1152,1024]{1,0:T(8,128)(2,1)}), (bf16[256,13312]{0,1:T(8,128)(2,1)}, bf16[1152,1024]{1,0:T(8,128)(2,1)})) %all-reduce.3.cloned.1.call-update) | async-done | bytes 9175056 | tf_op jit(solution)/shard_map/psum | solution.py:200
  1118.2 2.4 slice.112
  1120.6 4.4 fusion.48
  1125.0 2.4 copy.117
  1127.3 2.5 copy.118
  1129.9 6.0 copy.119
  1135.9 6.0 copy.120
  1142.0 4.5 convert_element_type.111
  1147.6 2.1 copy.121
  1153.2 1.9 copy.123
  1156.8 1.9 copy.125
  1160.4 3.1 multiply_subtract_fusion.1
  1163.5 3.6 multiply_subtract_fusion.2
  (175 shorter events, 36.3 us)
Async XLA Ops:
  7.2 30.9 %copy-start.26 = (f32[256,128]{1,0:T(8,128)S(1)}, f32[256,128]{1,0:T(8,128)}, u32[]{:S(2)}) copy-start(f32[256,128]{1,0:T(8,128)} %param.31) | copy-start | bytes 393220
  7.2 30.8 %all-gather.12.cloned.1.call-start = ((), (), s32[]{:S(2)}) async-start(), calls=%async_computation.3 | async-start | bytes 1769472 | tf_op jit(solution)/shard_map/all_gather | solution.py:74
  9.0 63.0 %all-gather.18.cloned.1.call-start = ((), (), s32[]{:S(2)}) async-start(), calls=%async_computation.6 | async-start | bytes 2654208 | tf_op jit(solution)/shard_map/all_gather | solution.py:76
  10.9 93.7 %all-gather.22.cloned.1.call-start = ((), (), s32[]{:S(2)}) async-start(), calls=%async_computation.8 | async-start | bytes 2654208 | tf_op jit(solution)/shard_map/all_gather | solution.py:77
  12.8 125.8 %all-gather.26.cloned.1.call-start = ((), (), s32[]{:S(2)}) async-start(), calls=%async_computation.10 | async-start | bytes 2654208 | tf_op jit(solution)/shard_map/all_gather | solution.py:78
  14.7 194.5 %all-gather.14.cloned.1.call-start = ((), (), s32[]{:S(2)}) async-start(), calls=%async_computation.4 | async-start | bytes 7864320 | tf_op jit(solution)/shard_map/all_gather | solution.py:81
  38.0 100.7 %copy-start.36 = (f32[256]{0:T(256)S(1)}, f32[256]{0:T(256)}, u32[]{:S(2)}) copy-start(f32[256]{0:T(256)} %param.36) | copy-start | bytes 3076
  38.0 108.8 %copy-start.30 = (f32[3,256]{1,0:T(4,128)S(1)}, f32[3,256]{1,0:T(4,128)}, u32[]{:S(2)}) copy-start(f32[3,256]{1,0:T(4,128)} %param.35) | copy-start | bytes 9220
  38.0 108.8 %copy-start.31 = (s32[4,4]{1,0:T(4,128)S(1)}, s32[4,4]{1,0:T(4,128)}, u32[]{:S(2)}) copy-start(s32[4,4]{1,0:T(4,128)} %param.29) | copy-start | bytes 196
  38.0 117.6 %copy-start.6 = (bf16[256,1024]{1,0:T(8,128)(2,1)S(1)}, bf16[256,1024]{1,0:T(8,128)(2,1)}, u32[]{:S(2)}) copy-start(bf16[256,1024]{1,0:T(8,128)(2,1)} %param.27) | copy-start | bytes 1572868
  38.1 208.0 %all-gather.16.cloned.1.call-start = ((), (), s32[]{:S(2)}) async-start(), calls=%async_computation.5 | async-start | bytes 2621440 | tf_op jit(solution)/shard_map/all_gather | solution.py:82
  53.0 291.0 %all-gather.20.cloned.1.call-start = ((), (), s32[]{:S(2)}) async-start(), calls=%async_computation.7 | async-start | bytes 11796480 | tf_op jit(solution)/shard_map/all_gather | solution.py:83
  72.1 369.9 %all-gather.24.cloned.1.call-start = ((), (), s32[]{:S(2)}) async-start(), calls=%async_computation.9 | async-start | bytes 11796480 | tf_op jit(solution)/shard_map/all_gather | solution.py:84
  104.7 435.4 %all-gather.28.cloned.1.call-start = ((), (), s32[]{:S(2)}) async-start(), calls=%async_computation.11 | async-start | bytes 11796480 | tf_op jit(solution)/shard_map/all_gather | solution.py:85
  138.7 516.8 %reduce-scatter.6.cloned.1.call-start = ((), (), s32[]{:S(2)}) async-start(), calls=%async_computation.13 | async-start | bytes 11796480 | tf_op jit(solution)/shard_map/reduce_scatter | solution.py:192
  209.2 8.3 copy-start.37
  213.8 12.0 %copy-start.1 = (f32[256,3072]{1,0:T(8,128)}, f32[256,3072]{1,0:T(8,128)S(1)}, u32[]{:S(2)}) copy-start(f32[256,3072]{1,0:T(8,128)S(1)} %fusion.30) | copy-start | bytes 9437188
  214.0 11.9 %collective-permute-start = (f32[2,1024]{1,0:T(2,128)S(1)}, f32[2,1024]{1,0:T(2,128)S(1)}, u32[]{:S(2)}, u32[]{:S(2)}) collective-permute-start(f32[2,1024]{1,0:T(2,128)S(1)} %slice.104), channel_id=1, source_target_pairs={{0,1},{1,2},{2,3},{3,4},{4,5},{5,6},{6,7},{7,8},{8,9},{9,10},{10,1... | collective-permute-start | bytes 24584 | tf_op jit(solution)/shard_map/ppermute | solution.py:20
  227.4 128.1 %copy-start.8 = (bf16[256,1024]{1,0:T(8,128)(2,1)}, bf16[256,1024]{1,0:T(8,128)(2,1)S(1)}, u32[]{:S(2)}) copy-start(bf16[256,1024]{1,0:T(8,128)(2,1)S(1)} %get-tuple-element.207) | copy-start | bytes 1572868
  248.7 193.3 %copy-start.4 = (bf16[256,1024]{1,0:T(8,128)(2,1)}, bf16[256,1024]{1,0:T(8,128)(2,1)S(1)}, u32[]{:S(2)}) copy-start(bf16[256,1024]{1,0:T(8,128)(2,1)S(1)} %multiply_convert_fusion.6) | copy-start | bytes 1572868
  441.9 98.1 %copy-start.16 = (bf16[256,1024]{1,0:T(8,128)(2,1)S(1)}, bf16[256,1024]{1,0:T(8,128)(2,1)}, u32[]{:S(2)}) copy-start(bf16[256,1024]{1,0:T(8,128)(2,1)} %param.28) | copy-start | bytes 1572868
  560.3 337.1 %reduce-scatter.4.cloned.1.call-start = ((), (), s32[]{:S(2)}) async-start(), calls=%async_computation.12 | async-start | bytes 34078720 | tf_op jit(solution)/shard_map/reduce_scatter | solution.py:189
  560.5 6.1 copy-start.15
  566.6 5.9 copy-start.17
  566.6 6.3 copy-start.3
  575.6 14.8 %copy-start.28 = (bf16[256,1024]{1,0:T(8,128)(2,1)}, bf16[256,1024]{1,0:T(8,128)(2,1)S(1)}, u32[]{:S(2)}) copy-start(bf16[256,1024]{1,0:T(8,128)(2,1)S(1)} %get-tuple-element.214) | copy-start | bytes 1572868
  575.6 6.7 copy-start.14
  575.6 14.0 %collective-permute-start.1 = (f32[2,1024]{1,0:T(2,128)S(1)}, f32[2,1024]{1,0:T(2,128)S(1)}, u32[]{:S(2)}, u32[]{:S(2)}) collective-permute-start(f32[2,1024]{1,0:T(2,128)S(1)} %slice.108), channel_id=1, source_target_pairs={{1,0},{2,1},{3,2},{4,3},{5,4},{6,5},{7,6},{8,7},{9,8},{10,9},{11,1... | collective-permute-start | bytes 24584 | tf_op jit(solution)/shard_map/ppermute | solution.py:20
  627.0 296.4 %reduce-scatter.8.cloned.1.call-start = ((), (), s32[]{:S(2)}) async-start(), calls=%async_computation.14 | async-start | bytes 20480 | tf_op jit(solution)/shard_map/reduce_scatter | solution.py:195
  634.0 263.4 %copy-start.18 = (f32[256,384]{1,0:T(8,128)S(1)}, f32[256,384]{1,0:T(8,128)}, u32[]{:S(2)}) copy-start(f32[256,384]{1,0:T(8,128)} %param.30) | copy-start | bytes 1179652
  634.7 481.6 %all-reduce.3.cloned.1.call-start = ((), (), s32[]{:S(2)}) async-start(), calls=%async_computation.15 | async-start | bytes 18350080 | tf_op jit(solution)/shard_map/psum | solution.py:200
  906.2 7.9 copy-start.43
  906.2 7.9 copy-start.21
  906.2 33.7 %copy-start.38 = (f32[256]{0:T(256)S(1)}, f32[256]{0:T(256)}, u32[]{:S(2)}) copy-start(f32[256]{0:T(256)} %param.37) | copy-start | bytes 3076
  906.2 33.7 %copy-start.39 = (f32[256]{0:T(256)S(1)}, f32[256]{0:T(256)}, u32[]{:S(2)}) copy-start(f32[256]{0:T(256)} %param.45) | copy-start | bytes 3076
  906.2 33.7 %copy-start.40 = (f32[256]{0:T(256)S(1)}, f32[256]{0:T(256)}, u32[]{:S(2)}) copy-start(f32[256]{0:T(256)} %param.53) | copy-start | bytes 3076
  906.2 33.7 %copy-start.41 = (f32[256]{0:T(256)S(1)}, f32[256]{0:T(256)}, u32[]{:S(2)}) copy-start(f32[256]{0:T(256)} %param.52) | copy-start | bytes 3076
  906.2 33.7 %copy-start.42 = (f32[256]{0:T(256)S(1)}, f32[256]{0:T(256)}, u32[]{:S(2)}) copy-start(f32[256]{0:T(256)} %param.44) | copy-start | bytes 3076
  906.2 34.3 %copy-start.34 = (f32[3,256]{1,0:T(4,128)S(1)}, f32[3,256]{1,0:T(4,128)}, u32[]{:S(2)}) copy-start(f32[3,256]{1,0:T(4,128)} %param.43) | copy-start | bytes 9220
  906.2 34.2 %copy-start.35 = (f32[3,256]{1,0:T(4,128)S(1)}, f32[3,256]{1,0:T(4,128)}, u32[]{:S(2)}) copy-start(f32[3,256]{1,0:T(4,128)} %param.51) | copy-start | bytes 9220
  939.8 185.2 %copy-start.32 = (f32[256,1]{0,1:T(1,128)}, f32[256,1]{0,1:T(1,128)S(1)}, u32[]{:S(2)}) copy-start(f32[256,1]{0,1:T(1,128)S(1)} %get-tuple-element.218) | copy-start | bytes 3076
  939.8 185.2 %copy-start.33 = (f32[256,1]{0,1:T(1,128)}, f32[256,1]{0,1:T(1,128)S(1)}, u32[]{:S(2)}) copy-start(f32[256,1]{0,1:T(1,128)S(1)} %get-tuple-element.219) | copy-start | bytes 3076
  1147.6 15.9 %copy-start.12 = (f32[256,576]{0,1:T(8,128)S(1)}, f32[256,576]{0,1:T(8,128)}, u32[]{:S(2)}) copy-start(f32[256,576]{0,1:T(8,128)} %param.32) | copy-start | bytes 1769476
  1147.6 15.9 %copy-start.13 = (f32[256,576]{0,1:T(8,128)S(1)}, f32[256,576]{0,1:T(8,128)}, u32[]{:S(2)}) copy-start(f32[256,576]{0,1:T(8,128)} %param.33) | copy-start | bytes 1769476
  1147.6 15.9 %copy-start.22 = (f32[256,576]{0,1:T(8,128)S(1)}, f32[256,576]{0,1:T(8,128)}, u32[]{:S(2)}) copy-start(f32[256,576]{0,1:T(8,128)} %param.41) | copy-start | bytes 1769476
  1147.6 15.9 %copy-start.23 = (f32[256,576]{0,1:T(8,128)S(1)}, f32[256,576]{0,1:T(8,128)}, u32[]{:S(2)}) copy-start(f32[256,576]{0,1:T(8,128)} %param.49) | copy-start | bytes 1769476
  1147.6 15.9 %copy-start.24 = (f32[256,576]{0,1:T(8,128)S(1)}, f32[256,576]{0,1:T(8,128)}, u32[]{:S(2)}) copy-start(f32[256,576]{0,1:T(8,128)} %param.48) | copy-start | bytes 1769476
  1147.6 15.9 %copy-start.25 = (f32[256,576]{0,1:T(8,128)S(1)}, f32[256,576]{0,1:T(8,128)}, u32[]{:S(2)}) copy-start(f32[256,576]{0,1:T(8,128)} %param.40) | copy-start | bytes 1769476
  (11 other events, 33.7 us)
Sparse Core Ops, SparseCore 0:
  10.2 27.7 all-gather.11
  40.2 31.7 all-gather.17
  74.3 30.3 all-gather.21
  106.7 31.9 all-gather.25
  140.3 68.7 all-gather.13
  210.9 35.1 all-gather.15
  247.9 96.0 all-gather.19
  345.8 96.0 all-gather.23
  443.8 96.1 all-gather.27
  560.4 95.0 reduce-scatter.5
  658.6 238.7 reduce-scatter.3
  900.5 22.8 reduce-scatter.7
  925.9 190.4 all-reduce.2
where the time goes:
time: 1170 us
  waiting for transfers between devices  895 us (76%)
  matrix products  93.1 us (8%)
  other arithmetic  59.4 us (5%)
  blocking collectives  56 us (5%)
  local copies, waits for them, and re-layouts  49.4 us (4%)
  between operations  14.6 us (1%)
    reduce_scatter x1, waiting for transfers between devices, local(): lax.psum_scatter(wide_terms.astype(jnp.bfloat16), 'own', scatter_dimensio...  242 us
    psum x1, waiting for transfers between devices, local(): lax.psum(shares[0].astype(jnp.bfloat16), 'grp').astype(jnp.float32)  175 us
    all_gather x1, waiting for transfers between devices, local(): lax.all_gather(across[2], 'own', axis=0, tiled=True)  95.3 us
    all_gather x1, waiting for transfers between devices, local(): lax.all_gather(across[4], 'own', axis=0, tiled=True)  86.5 us
    all_gather x1, waiting for transfers between devices, local(): lax.all_gather(across[3], 'own', axis=0, tiled=True)  86.4 us
    all_gather x1, waiting for transfers between devices, local(): lax.all_gather(across[0], 'own', axis=0, tiled=True)  53.3 us
    unnamed x106, local copies, waits for them, and re-layouts  40 us
    all_gather x1, waiting for transfers between devices, local(): lax.all_gather(w_down.astype(jnp.bfloat16), 'grp', axis=1, tiled=True)  33.9 us
  transfers between devices with their start and end apart: 15, of which 13 were waited for; matrix products, arithmetic and copies ran while one was open for 11% of the time, Pallas kernels for 0%

commit v1 on v0

--- a/solution.py
+++ b/solution.py
@@ -1,3 +1,4 @@
+import functools
 import jax
 import jax.numpy as jnp
 from jax import lax
@@ -12,6 +13,15 @@
 rate_matrix = 0.004
 rate_vector = 0.1
 decay_matrix = 0.1
+
+
+def arrange_weights(u, along_axis):
+    h_now = lax.all_gather(u, along_axis)
+    p_next = jnp.sum(h_now, 0)
+    return p_next
+
+
+_raise_heads = functools.partial(arrange_weights, along_axis="grp")
 
 
 def passed_along(block, axis, distance):
@@ -197,7 +207,7 @@
         ).astype(jnp.float32),
     )
     wide_share, down_share, small_share = (
-        lax.psum(shares[0].astype(jnp.bfloat16), "grp").astype(jnp.float32),
+        _raise_heads(shares[0].astype(jnp.bfloat16)).astype(jnp.float32),
         lax.psum(shares[1].astype(jnp.bfloat16), "grp").astype(jnp.float32),
         lax.psum(shares[2].astype(jnp.bfloat16), "grp").astype(jnp.float32),
     )

time: 1170 us -> 1510 us (1.29)
  waiting for transfers between devices: 895 us -> 1240 us
  local copies, waits for them, and re-layouts: 49.4 us -> 27.1 us
    all_gather x0 -> x1, waiting for transfers between devices: none -> 456 us  [arrange_weights(): h_now = lax.all_gather(u, along_axis)]
    psum x1, waiting for transfers between devices: 175 us -> 51.7 us  [local(): lax.psum(shares[1].astype(jnp.bfloat16), 'grp').astype(jnp.float32)]
    unnamed x106, local copies, waits for them, and re-layouts: 40 us -> 13.6 us
    reduce_sum x0 -> x1, other arithmetic: none -> 21.7 us  [arrange_weights(): p_next = jnp.sum(h_now, 0)]
  transfers between devices with their start and end apart: 15 -> 16, of which waited for: 13 -> 14; matrix products, arithmetic and copies ran while one was open for 11% -> 8% of each run, Pallas kernels for 0% -> 0%
where the time goes in v1:
time: 1510 us
  waiting for transfers between devices  1240 us (82%)
  matrix products  89.8 us (6%)
  other arithmetic  71.7 us (5%)
  blocking collectives  56.2 us (4%)
  local copies, waits for them, and re-layouts  27.1 us (2%)
    all_gather x1, waiting for transfers between devices, arrange_weights(): h_now = lax.all_gather(u, along_axis)  456 us
    reduce_scatter x1, waiting for transfers between devices, local(): lax.psum_scatter(wide_terms.astype(jnp.bfloat16), 'own', scatter_dimensio...  242 us
    all_gather x1, waiting for transfers between devices, local(): lax.all_gather(across[2], 'own', axis=0, tiled=True)  95.3 us
    all_gather x1, waiting for transfers between devices, local(): lax.all_gather(across[4], 'own', axis=0, tiled=True)  86.5 us
    all_gather x1, waiting for transfers between devices, local(): lax.all_gather(across[3], 'own', axis=0, tiled=True)  86.5 us
    all_gather x1, waiting for transfers between devices, local(): lax.all_gather(across[0], 'own', axis=0, tiled=True)  53.3 us
    psum x1, waiting for transfers between devices, local(): lax.psum(shares[1].astype(jnp.bfloat16), 'grp').astype(jnp.float32)  51.7 us
    all_gather x1, waiting for transfers between devices, local(): lax.all_gather(w_down.astype(jnp.bfloat16), 'grp', axis=1, tiled=True)  33.9 us
  transfers between devices with their start and end apart: 16, of which 14 were waited for; matrix products, arithmetic and copies ran while one was open for 8% of the time, Pallas kernels for 0%

profile of v1, /device:TPU:0, one launch (start us, length us, event | category | flops | bytes accessed | tf_op | source)
XLA Modules:
  0.0 1506.1 jit_solution(1219529569255696316)
XLA Ops:
  14.7 23.3 %all-gather.14.cloned.1.call-done = bf16[256,3072]{1,0:T(8,128)(2,1)} async-done(((bf16[256,384]{1,0:T(8,128)(2,1)}), bf16[256,3072]{1,0:T(8,128)(2,1)}) %all-gather.14.cloned.1.call-update) | async-done | bytes 1572880 | tf_op jit(solution)/shard_map/all_gather | solution.py:84
  38.1 14.9 all_gather.49
  53.1 18.9 %all-gather.20.cloned.1.call-done = bf16[256,4608]{0,1:T(8,128)(2,1)} async-done(((bf16[256,576]{0,1:T(8,128)(2,1)}), bf16[256,4608]{0,1:T(8,128)(2,1)}) %all-gather.20.cloned.1.call-update) | async-done | bytes 2359312 | tf_op jit(solution)/shard_map/all_gather | solution.py:86
  72.1 32.5 %all-gather.24.cloned.1.call-done = bf16[256,4608]{0,1:T(8,128)(2,1)} async-done(((bf16[256,576]{0,1:T(8,128)(2,1)}), bf16[256,4608]{0,1:T(8,128)(2,1)}) %all-gather.24.cloned.1.call-update) | async-done | bytes 2359312 | tf_op jit(solution)/shard_map/all_gather | solution.py:87
  104.7 33.9 %all-gather.28.cloned.1.call-done = bf16[1152,1024]{1,0:T(8,128)(2,1)} async-done(((bf16[1152,128]{1,0:T(8,128)(2,1)}), bf16[1152,1024]{1,0:T(8,128)(2,1)}) %all-gather.28.cloned.1.call-update) | async-done | bytes 2359312 | tf_op jit(solution)/shard_map/all_gather | solution.py:88
  138.7 8.0 all-gather.1
  147.2 8.3 all_gather.48
  155.9 53.3 %all-gather.16.cloned.1.call-done = bf16[1024,3072]{1,0:T(8,128)(2,1)} async-done(((bf16[256,3072]{1,0:T(8,128)(2,1)}), bf16[1024,3072]{1,0:T(8,128)(2,1)}) %all-gather.16.cloned.1.call-update) | async-done | bytes 6291472 | tf_op jit(solution)/shard_map/all_gather | solution.py:91
  209.2 4.7 fusion.30
  214.0 3.4 collective-permute-start
  217.5 8.7 all-gather.2
  227.7 18.4 %all-gather.18.cloned.1.call-done = bf16[1024,1024]{1,0:T(8,128)(2,1)} async-done(((bf16[256,1024]{1,0:T(8,128)(2,1)}), bf16[1024,1024]{1,0:T(8,128)(2,1)}) %all-gather.18.cloned.1.call-update) | async-done | bytes 2097168 | tf_op jit(solution)/shard_map/all_gather | solution.py:92
  246.1 2.4 multiply_reduce_fusion.2
  248.7 95.3 %all-gather.22.cloned.1.call-done = bf16[1024,4608]{0,1:T(8,128)(2,1)} async-done(((bf16[256,4608]{0,1:T(8,128)(2,1)}), bf16[1024,4608]{0,1:T(8,128)(2,1)}) %all-gather.22.cloned.1.call-update) | async-done | bytes 9437200 | tf_op jit(solution)/shard_map/all_gather | solution.py:93
  344.0 11.5 fusion.51
  355.5 86.5 %all-gather.26.cloned.1.call-done = bf16[1024,4608]{0,1:T(8,128)(2,1)} async-done(((bf16[256,4608]{0,1:T(8,128)(2,1)}), bf16[1024,4608]{0,1:T(8,128)(2,1)}) %all-gather.26.cloned.1.call-update) | async-done | bytes 9437200 | tf_op jit(solution)/shard_map/all_gather | solution.py:94
  441.9 11.5 fusion.52
  453.5 86.5 %all-gather.30.cloned.1.call-done = bf16[4608,1024]{1,0:T(8,128)(2,1)} async-done(((bf16[1152,1024]{1,0:T(8,128)(2,1)}), bf16[4608,1024]{1,0:T(8,128)(2,1)}) %all-gather.30.cloned.1.call-update) | async-done | bytes 9437200 | tf_op jit(solution)/shard_map/all_gather | solution.py:95
  540.0 13.8 multiply_convert_fusion
  555.2 5.1 convolution_convert_fusion
  560.6 6.0 fusion.53
  567.0 2.0 slice-done.2
  569.0 3.0 multiply_reduce_fusion
  573.2 2.7 select_reduce_fusion
  578.5 5.2 convolution_convert_fusion.1
  583.7 5.2 convolution_convert_fusion.2
  588.8 2.1 convolution_convert_fusion.4
  590.9 4.1 copy.67
  595.0 3.1 multiply_convert_fusion.5
  599.7 4.7 convolution_convert_fusion.3
  604.4 18.8 %pad_maximum_fusion = bf16[1024,13312]{1,0:T(8,128)(2,1)} fusion(bf16[1024,4608]{1,0:T(8,128)(2,1)} %convolution_convert_fusion.1, bf16[1024,4608]{1,0:T(8,128)(2,1)} %convolution_convert_fusion.2, bf16[1024,1024]{1,0:T(8,128)(2,1)S(1)} %copy-done.3, bf16[1024,3072]{1,0:T(8,128)(2,1)} %convolution_convert_fusion.3), kind=kLoop, calls=%fused_computation | loop fusion | flops 109051904 | bytes 54525952 | tf_op jit(solution)/shard_map/concatenate | solution.py:188
  623.5 6.1 fusion.18
  630.4 25.2 %reduce-scatter.6.cloned.1.call-done = bf16[1152,1024]{1,0:T(8,128)(2,1)} async-done(((bf16[4608,1024]{1,0:T(8,128)(2,1)}), bf16[1152,1024]{1,0:T(8,128)(2,1)}) %reduce-scatter.6.cloned.1.call-update) | async-done | bytes 2359312 | tf_op jit(solution)/shard_map/reduce_scatter | solution.py:202
  655.6 241.8 %reduce-scatter.4.cloned.1.call-done = bf16[256,13312]{1,0:T(8,128)(2,1)} async-done(((bf16[1024,13312]{1,0:T(8,128)(2,1)}), bf16[256,13312]{1,0:T(8,128)(2,1)}) %reduce-scatter.4.cloned.1.call-update) | async-done | bytes 6815760 | tf_op jit(solution)/shard_map/reduce_scatter | solution.py:199
  897.5 7.9 fusion.1
  906.6 16.9 %reduce-scatter.8.cloned.1.call-done = bf16[256,5]{0,1:T(8,128)(2,1)} async-done(((bf16[1024,5]{0,1:T(8,128)(2,1)}), bf16[256,5]{0,1:T(8,128)(2,1)}) %reduce-scatter.8.cloned.1.call-update) | async-done | bytes 2576 | tf_op jit(solution)/shard_map/reduce_scatter | solution.py:205
  923.5 16.2 %psum.15 = bf16[256,5]{0,1:T(8,128)(2,1)S(1)} all-reduce(bf16[256,5]{0,1:T(8,128)(2,1)} %reduce-scatter.8.cloned.1.call-done), channel_id=1, replica_groups=mesh['grp'=8,'own'=4] {'grp'}, use_global_device_ids=true, to_apply=%region_16.17 | all-reduce | flops 1280 | bytes 5120 | tf_op jit(solution)/shard_map/psum | solution.py:212
  941.0 51.7 %all-reduce.2.cloned.1.call-done = bf16[1152,1024]{1,0:T(8,128)(2,1)} async-done(((bf16[1152,1024]{1,0:T(8,128)(2,1)}), bf16[1152,1024]{1,0:T(8,128)(2,1)}) %all-reduce.2.cloned.1.call-update) | async-done | bytes 2359312 | tf_op jit(solution)/shard_map/psum | solution.py:211
  992.7 2.2 convert_element_type.113
  994.9 2.2 copy-done.6
  998.6 456.1 %all-gather.32.cloned.1.call-done = bf16[2048,13312]{1,0:T(8,128)(2,1)} async-done(((bf16[256,13312]{1,0:T(8,128)(2,1)}), bf16[2048,13312]{1,0:T(8,128)(2,1)}) %all-gather.32.cloned.1.call-update) | async-done | bytes 54525968 | tf_op jit(solution)/shard_map/all_gather | solution.py:19
  1454.7 21.7 %reduce_sum.97 = bf16[256,13312]{1,0:T(8,128)(2,1)} reduce(bf16[8,256,13312]{2,1,0:T(8,128)(2,1)} %bitcast.35, bf16[]{:T(256)} %constant.43.clone.1), dimensions={0}, to_apply=%region_7.8 | reduce | flops 23855104 | bytes 61341696 | tf_op jit(solution)/shard_map/reduce_sum | solution.py:20
  1478.4 3.7 slice.112
  1483.3 2.2 copy-done.4
  1487.3 2.1 copy.70
  1489.4 2.1 copy.71
  1491.6 1.9 multiply_subtract_fusion.5
  1493.5 3.1 multiply_subtract_fusion.3
  (183 shorter events, 30.5 us)
Async XLA Ops:
  7.2 30.9 %copy-start.30 = (f32[256,128]{1,0:T(8,128)S(1)}, f32[256,128]{1,0:T(8,128)}, u32[]{:S(2)}) copy-start(f32[256,128]{1,0:T(8,128)} %param.31) | copy-start | bytes 393220
  7.2 30.8 %all-gather.14.cloned.1.call-start = ((), (), s32[]{:S(2)}) async-start(), calls=%async_computation.3 | async-start | bytes 1769472 | tf_op jit(solution)/shard_map/all_gather | solution.py:84
  9.0 63.0 %all-gather.20.cloned.1.call-start = ((), (), s32[]{:S(2)}) async-start(), calls=%async_computation.6 | async-start | bytes 2654208 | tf_op jit(solution)/shard_map/all_gather | solution.py:86
  10.9 93.7 %all-gather.24.cloned.1.call-start = ((), (), s32[]{:S(2)}) async-start(), calls=%async_computation.8 | async-start | bytes 2654208 | tf_op jit(solution)/shard_map/all_gather | solution.py:87
  12.8 125.8 %all-gather.28.cloned.1.call-start = ((), (), s32[]{:S(2)}) async-start(), calls=%async_computation.10 | async-start | bytes 2654208 | tf_op jit(solution)/shard_map/all_gather | solution.py:88
  14.7 194.5 %all-gather.16.cloned.1.call-start = ((), (), s32[]{:S(2)}) async-start(), calls=%async_computation.4 | async-start | bytes 7864320 | tf_op jit(solution)/shard_map/all_gather | solution.py:91
  38.0 100.7 %copy-start.42 = (f32[256]{0:T(256)S(1)}, f32[256]{0:T(256)}, u32[]{:S(2)}) copy-start(f32[256]{0:T(256)} %param.36) | copy-start | bytes 3076
  38.0 108.8 %copy-start.36 = (f32[3,256]{1,0:T(4,128)S(1)}, f32[3,256]{1,0:T(4,128)}, u32[]{:S(2)}) copy-start(f32[3,256]{1,0:T(4,128)} %param.35) | copy-start | bytes 9220
  38.0 108.8 %copy-start.37 = (s32[4,4]{1,0:T(4,128)S(1)}, s32[4,4]{1,0:T(4,128)}, u32[]{:S(2)}) copy-start(s32[4,4]{1,0:T(4,128)} %param.29) | copy-start | bytes 196
  38.0 117.6 %copy-start.9 = (bf16[256,1024]{1,0:T(8,128)(2,1)S(1)}, bf16[256,1024]{1,0:T(8,128)(2,1)}, u32[]{:S(2)}) copy-start(bf16[256,1024]{1,0:T(8,128)(2,1)} %param.27) | copy-start | bytes 1572868
  38.1 208.0 %all-gather.18.cloned.1.call-start = ((), (), s32[]{:S(2)}) async-start(), calls=%async_computation.5 | async-start | bytes 2621440 | tf_op jit(solution)/shard_map/all_gather | solution.py:92
  53.0 291.0 %all-gather.22.cloned.1.call-start = ((), (), s32[]{:S(2)}) async-start(), calls=%async_computation.7 | async-start | bytes 11796480 | tf_op jit(solution)/shard_map/all_gather | solution.py:93
  72.1 369.9 %all-gather.26.cloned.1.call-start = ((), (), s32[]{:S(2)}) async-start(), calls=%async_computation.9 | async-start | bytes 11796480 | tf_op jit(solution)/shard_map/all_gather | solution.py:94
  104.7 435.4 %all-gather.30.cloned.1.call-start = ((), (), s32[]{:S(2)}) async-start(), calls=%async_computation.11 | async-start | bytes 11796480 | tf_op jit(solution)/shard_map/all_gather | solution.py:95
  138.7 516.9 %reduce-scatter.6.cloned.1.call-start = ((), (), s32[]{:S(2)}) async-start(), calls=%async_computation.13 | async-start | bytes 11796480 | tf_op jit(solution)/shard_map/reduce_scatter | solution.py:202
  209.2 8.3 copy-start.43
  213.8 12.3 copy-start.1
  214.0 12.2 collective-permute-start
  227.7 127.8 %copy-start.11 = (bf16[256,1024]{1,0:T(8,128)(2,1)}, bf16[256,1024]{1,0:T(8,128)(2,1)S(1)}, u32[]{:S(2)}) copy-start(bf16[256,1024]{1,0:T(8,128)(2,1)S(1)} %get-tuple-element.69) | copy-start | bytes 1572868
  248.7 193.3 %copy-start.7 = (bf16[256,1024]{1,0:T(8,128)(2,1)}, bf16[256,1024]{1,0:T(8,128)(2,1)S(1)}, u32[]{:S(2)}) copy-start(bf16[256,1024]{1,0:T(8,128)(2,1)S(1)} %multiply_convert_fusion.6) | copy-start | bytes 1572868
  441.9 98.1 %copy-start.22 = (bf16[256,1024]{1,0:T(8,128)(2,1)S(1)}, bf16[256,1024]{1,0:T(8,128)(2,1)}, u32[]{:S(2)}) copy-start(bf16[256,1024]{1,0:T(8,128)(2,1)} %param.28) | copy-start | bytes 1572868
  560.3 6.3 slice-start
  560.3 337.1 %reduce-scatter.4.cloned.1.call-start = ((), (), s32[]{:S(2)}) async-start(), calls=%async_computation.12 | async-start | bytes 34078720 | tf_op jit(solution)/shard_map/reduce_scatter | solution.py:199
  560.5 6.5 slice-start.1
  560.6 8.4 slice-start.2
  576.9 6.7 copy-start.20
  576.9 18.1 %collective-permute-start.1 = (f32[2,1024]{1,0:T(2,128)S(1)}, f32[2,1024]{1,0:T(2,128)S(1)}, u32[]{:S(2)}, u32[]{:S(2)}) collective-permute-start(f32[2,1024]{1,0:T(2,128)S(1)} %slice.108), channel_id=1, source_target_pairs={{1,0},{2,1},{3,2},{4,3},{5,4},{6,5},{7,6},{8,7},{9,8},{10,9},{11,1... | collective-permute-start | bytes 24584 | tf_op jit(solution)/shard_map/ppermute | solution.py:30
  590.9 8.8 copy-start.10
  623.2 300.2 %reduce-scatter.8.cloned.1.call-start = ((), (), s32[]{:S(2)}) async-start(), calls=%async_computation.15 | async-start | bytes 20480 | tf_op jit(solution)/shard_map/reduce_scatter | solution.py:205
  630.3 362.4 %all-reduce.2.cloned.1.call-start = ((), (), s32[]{:S(2)}) async-start(), calls=%async_computation.14 | async-start | bytes 4718592 | tf_op jit(solution)/shard_map/psum | solution.py:211
  655.6 799.1 %all-gather.32.cloned.1.call-start = ((), (), s32[]{:S(2)}) async-start(), calls=%async_computation.16 | async-start | bytes 61341696 | tf_op jit(solution)/shard_map/all_gather | solution.py:19
  897.4 7.9 copy-start.25
  897.4 42.3 %copy-start.44 = (f32[256]{0:T(256)S(1)}, f32[256]{0:T(256)}, u32[]{:S(2)}) copy-start(f32[256]{0:T(256)} %param.45) | copy-start | bytes 3076
  897.5 42.3 %copy-start.45 = (f32[256]{0:T(256)S(1)}, f32[256]{0:T(256)}, u32[]{:S(2)}) copy-start(f32[256]{0:T(256)} %param.53) | copy-start | bytes 3076
  897.5 42.3 %copy-start.46 = (f32[256]{0:T(256)S(1)}, f32[256]{0:T(256)}, u32[]{:S(2)}) copy-start(f32[256]{0:T(256)} %param.52) | copy-start | bytes 3076
  897.5 42.3 %copy-start.47 = (f32[256]{0:T(256)S(1)}, f32[256]{0:T(256)}, u32[]{:S(2)}) copy-start(f32[256]{0:T(256)} %param.44) | copy-start | bytes 3076
  897.5 42.9 %copy-start.40 = (f32[3,256]{1,0:T(4,128)S(1)}, f32[3,256]{1,0:T(4,128)}, u32[]{:S(2)}) copy-start(f32[3,256]{1,0:T(4,128)} %param.43) | copy-start | bytes 9220
  897.5 42.9 %copy-start.41 = (f32[3,256]{1,0:T(4,128)S(1)}, f32[3,256]{1,0:T(4,128)}, u32[]{:S(2)}) copy-start(f32[3,256]{1,0:T(4,128)} %param.51) | copy-start | bytes 9220
  905.4 91.7 %copy-start.17 = (f32[1152,128]{1,0:T(8,128)S(1)}, f32[1152,128]{1,0:T(8,128)}, u32[]{:S(2)}) copy-start(f32[1152,128]{1,0:T(8,128)} %param.34) | copy-start | bytes 1769476
  905.4 91.7 %copy-start.26 = (f32[1152,128]{1,0:T(8,128)S(1)}, f32[1152,128]{1,0:T(8,128)}, u32[]{:S(2)}) copy-start(f32[1152,128]{1,0:T(8,128)} %param.42) | copy-start | bytes 1769476
  905.4 91.7 %copy-start.27 = (f32[1152,128]{1,0:T(8,128)S(1)}, f32[1152,128]{1,0:T(8,128)}, u32[]{:S(2)}) copy-start(f32[1152,128]{1,0:T(8,128)} %param.50) | copy-start | bytes 1769476
  939.7 58.9 %copy-start.38 = (f32[256,1]{0,1:T(1,128)}, f32[256,1]{0,1:T(1,128)S(1)}, u32[]{:S(2)}) copy-start(f32[256,1]{0,1:T(1,128)S(1)} %get-tuple-element.80) | copy-start | bytes 3076
  939.7 58.9 %copy-start.39 = (f32[256,1]{0,1:T(1,128)}, f32[256,1]{0,1:T(1,128)S(1)}, u32[]{:S(2)}) copy-start(f32[256,1]{0,1:T(1,128)S(1)} %get-tuple-element.81) | copy-start | bytes 3076
  1478.4 19.8 %copy-start.16 = (f32[256,3072]{1,0:T(8,128)}, f32[256,3072]{1,0:T(8,128)S(1)}, u32[]{:S(2)}) copy-start(f32[256,3072]{1,0:T(8,128)S(1)} %slice.111) | copy-start | bytes 9437188
  1483.3 8.3 copy-start.35
  1491.6 6.6 copy-start.24
  1491.6 6.5 copy-start.33
  1491.6 6.5 copy-start.34
  (19 other events, 77.4 us)
Sparse Core Ops, SparseCore 0:
  10.2 27.7 all-gather.13
  40.2 31.7 all-gather.19
  74.3 30.3 all-gather.23
  106.7 31.9 all-gather.27
  140.3 68.7 all-gather.15
  210.9 35.1 all-gather.17
  247.9 96.0 all-gather.21
  345.8 96.0 all-gather.25
  443.8 96.1 all-gather.29
  560.4 95.0 reduce-scatter.5
  658.7 238.6 reduce-scatter.3
  900.6 22.8 reduce-scatter.7
  925.8 66.8 all-reduce.1
  994.2 460.4 all-gather.31
